TPU v7x, 32 devices: a whole 2x2x4 slice. The times are simulated.
32 devices in a mesh: groups: 2 (over y), date: 4 (over x, core), col: 4 (over z).
Axes of the slice: x: 2, y: 2, z: 4, core: 2. Of those that a mesh axis runs over, the one named last changes fastest.
Arguments:
- scenes: bfloat16 [16, 2, 128, 1024], P('date', None, 'groups', 'col'), parts along dimension 2, may hold values from -6 to 6
- pair_dates: int32 [96, 2], P('date'), may hold values from 0 to 15, as said below
- pair_count: int32 [4], P('date'), may hold values from 12 to 24, as said below
- inverse: float32 [15, 96], replicated, may hold values from -0.625 to 0.625
Outputs:
- series: float32 [15, 2, 64, 128], P(None, None, ('groups', 'date'), 'col'), parts along dimension 2
There are 2 independent parts, one for each index of `groups`. A program takes and returns all parts, laid end to end along the dimension named above; an argument that names none is the same for every part. Nothing has to cross between parts.
Inputs may be any that keep to these rules, and one draw needn't show every extreme that they name: `pair_dates`: each row names a reference acquisition and a later secondary one. Slots i * 24 to (i + 1) * 24 - 1 belong to owner i (index i of date); every slot of owner i names acquisitions held by indices i - 2 to i + 2 of date (as far as these exist), and one live pair of every owner names the lowest and the highest acquisition of that range. `pair_count`: entry i is the number of live slots of owner i; they come first in its block and the other slots are ignored. Some owner has all its slots live.
All inputs are finite; a program needn't handle non-finite values.
Results may differ from a plain program's by a relative error of at most 0.0003.
Values may be sent and summed in bfloat16 or wider, within the bound.
A program may use at most 64 MiB of HBM per device.

v0:
```python
import functools

import jax
import jax.numpy as jnp
from jax import lax
from jax.experimental import pallas as pl
from jax.experimental.pallas import tpu as pltpu
from jax.sharding import PartitionSpec as P

MESH = pl.DeviceIdType.MESH
F32 = jnp.float32
BF16 = jnp.bfloat16
EDGE = 4


def flipped(place, slot):
    bit = 1
    out = place
    while bit <= slot:
        if slot & bit:
            out = out + bit - 2 * bit * ((place // bit) % 2)
        bit *= 2
    return out


def split(value):
    high = value.astype(BF16)
    return high, (value - high.astype(F32)).astype(BF16)


def iota(shape, dim):
    return lax.broadcasted_iota(jnp.int32, shape, dim)


def stack_kernel(
    cfg,
    scenes, dates, count, inverse, out,
    local, base, dates_in, counts_in, edge_out, edge_in,
    raw, cells, h_high, h_low, weights, k_high, k_low, l_high, l_low,
    load_sem, send_sem, recv_sem, dates_send, dates_recv, count_send, count_recv, edge_send, edge_recv,
    inverse_in, own_sem,
):
    D, C, A, R, X, S, NP = (cfg[k] for k in ("D", "C", "A", "R", "X", "S", "NP"))
    dates_total = D * A
    T = X // 128
    TT = T + 1
    half = R // 2
    looks = X // 8
    block = A * A * half
    diag = block // 2
    date = lax.axis_index("date")
    col = lax.axis_index("col")
    has_left = col > 0
    has_right = col < C - 1

    barrier = pltpu.get_barrier_semaphore()
    for r in range(1, D):
        pl.semaphore_signal(barrier, inc=1, device_id={"date": flipped(date, r)}, device_id_type=MESH)

    @pl.when(has_left)
    def _():
        for r in range(D):
            pl.semaphore_signal(barrier, inc=1, device_id={"date": flipped(date, r), "col": col - 1}, device_id_type=MESH)

    @pl.when(has_right)
    def _():
        for r in range(D):
            pl.semaphore_signal(barrier, inc=1, device_id={"date": flipped(date, r), "col": col + 1}, device_id_type=MESH)

    load = pltpu.make_async_copy(scenes, local, load_sem)
    load.start()
    own = [
        pltpu.make_async_copy(dates, dates_in.at[date], own_sem.at[0]),
        pltpu.make_async_copy(count, counts_in.at[date], own_sem.at[1]),
        pltpu.make_async_copy(inverse, inverse_in, own_sem.at[2]),
    ]

    for copy in own:
        copy.start()

    load.wait()
    lane = iota((D * R, 128), 1)
    to_left = jnp.zeros((D * R, 128), F32)
    to_right = jnp.zeros((D * R, 128), F32)
    for i in range(2 * A):
        first = local[i // 2, i % 2, :, 0:128].astype(F32)
        last = local[i // 2, i % 2, :, X - 128:X].astype(F32)
        shift = (8 * i + EDGE) % 128
        to_left = jnp.where(lane // EDGE == 2 * i + 1, pltpu.roll(first, shift, 1), to_left)
        shift = (8 * i + EDGE) % 128
        to_right = jnp.where(lane // EDGE == 2 * i, pltpu.roll(last, shift, 1), to_right)
    edge_out[0] = to_right.astype(BF16)
    edge_out[1] = to_left.astype(BF16)

    @pl.when(jnp.logical_not(has_left))
    def _():
        edge_in[0] = jnp.zeros((D, R, 128), BF16)

    @pl.when(jnp.logical_not(has_right))
    def _():
        edge_in[1] = jnp.zeros((D, R, 128), BF16)

    pl.semaphore_wait(barrier, D - 1 + D * (has_left.astype(jnp.int32) + has_right.astype(jnp.int32)))

    def rows_of(place):
        return pl.ds(pl.multiple_of(place * R, R), R)

    def remote(src, dst, ssem, rsem, device):
        return pltpu.make_async_remote_copy(src_ref=src, dst_ref=dst, send_sem=ssem, recv_sem=rsem, device_id=device, device_id_type=MESH)

    to_next = {}
    order = list(range(D - 1, 0, -1))
    for r in range(1, D):
        there = flipped(date, r)
        to_next["dates", r] = remote(dates, dates_in.at[date], dates_send.at[r], dates_recv.at[r], {"date": there})
        to_next["count", r] = remote(count, counts_in.at[date], count_send.at[r], count_recv.at[r], {"date": there})
        to_next["scene", r] = remote(scenes.at[:, :, rows_of(there), :], base.at[r], send_sem.at[r], recv_sem.at[r], {"date": there})
    for r in range(D):
        there = flipped(date, r)
        to_next["right", r] = remote(edge_out.at[0, rows_of(there)], edge_in.at[0, r], edge_send.at[0, r], edge_recv.at[0, r], {"date": there, "col": col + 1})
        to_next["left", r] = remote(edge_out.at[1, rows_of(there)], edge_in.at[1, r], edge_send.at[1, r], edge_recv.at[1, r], {"date": there, "col": col - 1})
    for r in order:
        to_next["dates", r].start()
        to_next["count", r].start()

    @pl.when(has_right)
    def _():
        for r in order + [0]:
            to_next["right", r].start()

    @pl.when(has_left)
    def _():
        for r in order + [0]:
            to_next["left", r].start()

    for r in cfg["send_order"]:
        to_next["scene", r].start()

    row = iota((TT * 128, 128), 0)
    spot = row - TT * 128 + 128
    column = jnp.where(spot < 0, row, jnp.where(spot < EDGE, spot - EDGE, spot - EDGE + X))
    usable = (spot < 2 * EDGE)
    target = iota((TT * 128, 128), 1)
    for c in range(2):
        look = target - 64 * c
        offset = column - 8 * look + 4
        inside = usable & (look >= 0) & (look < looks) & (offset >= 0) & (offset < 16)
        value = jnp.where(inside, (8.0 - jnp.abs(offset.astype(F32) - 7.5)) / 128.0, 0.0)
        weights[c * TT * 128:(c + 1) * TT * 128, :] = value.astype(BF16)

    def unpack(slot, main):
        for c in range(2):
            for t in range(T):
                for i in range(A):
                    at = ((c * TT + t) * A + i) * R
                    raw[at:at + R, :] = main(i, c)[:, t * 128:(t + 1) * 128].astype(F32)
        edges = edge_in[0, slot].astype(F32) + edge_in[1, slot].astype(F32)
        for c in range(2):
            for i in range(A):
                at = ((c * TT + T) * A + i) * R
                shift = (128 - 8 * (2 * i + c)) % 128
                raw[at:at + R, :] = pltpu.roll(edges, shift, 1) if shift else edges
        total = 2 * TT * A * half
        for parity in range(2):
            got = raw[pl.ds(parity, total, stride=2), :]
            cells[parity, :, slot * A:(slot + 1) * A] = got.reshape(2 * TT, A, half, 128)

    def emit(at, pieces):
        rows = pieces[0][0].shape[0]
        for t, both in enumerate(pieces):
            for c in range(2):
                high, low = split(both[c])
                h_high[at:at + rows, (c * TT + t) * 128:(c * TT + t + 1) * 128] = high
                h_low[at:at + rows, (c * TT + t) * 128:(c * TT + t + 1) * 128] = low

    def product(p_of, s_of, t):
        real = imaginary = None
        for parity in range(2):
            p0, p1 = p_of(parity, t), p_of(parity, TT + t)
            s0, s1 = s_of(parity, t), s_of(parity, TT + t)
            one = p0 * s0 + p1 * s1
            two = p1 * s0 - p0 * s1
            real = one if real is None else real + one
            imaginary = two if imaginary is None else imaginary + two
        return real, imaginary

    def pair_order(ra, rb):
        bit = 1
        while 2 * bit <= (ra ^ rb):
            bit *= 2
        swap = (flipped(date, ra) // bit) % 2
        low = ra + swap * (rb - ra)
        high = rb - swap * (rb - ra)
        return low, high

    chunks = []

    def cross(ra, rb):
        at = len(chunks) * block
        chunks.append((ra, rb))
        low, high = pair_order(ra, rb)
        for i in range(A):
            pieces = []
            for t in range(TT):
                both = product(
                    lambda q, n: cells[q, n, low * A + i][None],
                    lambda q, n: cells[q, n, pl.ds(high * A, A)], t)
                pieces.append([v.reshape(A * half, 128) for v in both])
            emit(at + i * A * half, pieces)

    def within(ra):
        at = len(chunks) * block
        chunks.append((ra, ra + 1))
        for side in range(2):
            slot = ra + side
            pieces = []
            for t in range(TT):
                parts = [], []
                for step in range(1, A):
                    both = product(
                        lambda q, n: cells[q, n, slot * A:slot * A + A - step],
                        lambda q, n: cells[q, n, slot * A + step:slot * A + A], t)
                    for c in range(2):
                        parts[c].append(both[c].reshape((A - step) * half, 128))
                pad = jnp.zeros((diag - A * (A - 1) // 2 * half, 128), F32)
                pieces.append([jnp.concatenate(parts[c] + [pad], axis=0) for c in range(2)])
            emit(at + side * diag, pieces)

    def look(start, stop):
        rows = slice(start * block, stop * block)
        got = jnp.dot(h_high[rows, :], weights[...], preferred_element_type=F32)
        got = got + jnp.dot(h_low[rows, :], weights[...], preferred_element_type=F32)
        l_high[rows, :], l_low[rows, :] = split(got)

    def wait_edges(r):
        @pl.when(has_left)
        def _():
            to_next["right", r].wait_recv()

        @pl.when(has_right)
        def _():
            to_next["left", r].wait_recv()

    wait_edges(0)
    unpack(0, lambda i, c: local[i, c, rows_of(date), :])

    order_in = cfg["order_in"]
    looked = 0
    arrived = [0]
    for r in order_in:
        if r == order_in[0]:
            for copy in own:
                copy.wait()
            for q in range(1, D):
                to_next["dates", q].wait_recv()
                to_next["count", q].wait_recv()
        wait_edges(r)
        to_next["scene", r].wait_recv()
        unpack(r, lambda i, c: base[r, i, c])
        if (r ^ 1) in arrived:
            within(r & ~1)
        for other in arrived:
            cross(min(other, r), max(other, r))
        arrived.append(r)
        look(looked, len(chunks))
        looked = len(chunks)
        if r == order_in[0]:
            invert_matrix(cfg, date, dates_in, counts_in, inverse_in, k_high, k_low, pair_order)

    lh, ll = l_high[...], l_low[...]
    kh = k_high[...]
    series = jnp.dot(kh, lh, preferred_element_type=F32)
    series = series + jnp.dot(kh, ll, preferred_element_type=F32)
    series = series + jnp.dot(k_low[...], lh, preferred_element_type=F32)
    for c in range(2):
        out[:, c] = series[:, c * 64:c * 64 + looks].reshape(NP, half, looks)

    for r in range(1, D):
        for kind in ("dates", "count", "scene"):
            to_next[kind, r].wait_send()

    @pl.when(has_right)
    def _():
        for r in range(D):
            to_next["right", r].wait_send()

    @pl.when(has_left)
    def _():
        for r in range(D):
            to_next["left", r].wait_send()


def chunk_list(order_in):
    chunks, arrived = [], [0]
    for r in order_in:
        if (r ^ 1) in arrived:
            chunks.append((r & ~1, None))
        for other in arrived:
            chunks.append((min(other, r), max(other, r)))
        arrived.append(r)
    return chunks


def invert_matrix(cfg, date, dates_in, counts_in, inverse, k_high, k_low, pair_order):
    D, A, R, S, NP = (cfg[k] for k in ("D", "A", "R", "S", "NP"))
    half = R // 2
    block = A * A * half
    diag = block // 2
    total = D * A
    codes = []
    for d in range(D):
        row = dates_in[d, 0:1, :] * total + dates_in[d, 1:2, :]
        live = iota((1, S), 1) < counts_in[d]
        codes.append(jnp.where(live, row, -1).astype(F32))
    codes.append(jnp.full((8 - D % 8 if D % 8 else 8, S), -1.0, F32))
    table = jnp.concatenate(codes, axis=0)
    table = jnp.concatenate([table, jnp.full((table.shape[0], 128 - S), -1.0, F32)], axis=1)
    turned = jnp.transpose(table)
    code = jnp.concatenate([turned[0:S, d:d + 1] for d in range(D)], axis=0).astype(jnp.int32)
    inv = inverse[...]
    spread = jnp.broadcast_to(inv[:, None, :], (NP, half, D * S)).reshape(NP * half, D * S)
    spread_high, spread_low = split(spread)
    place = iota((1, block), 1)
    same = (iota((NP * half, block), 0) % half) == (iota((NP * half, block), 1) % half)
    for n, (ra, rb) in enumerate(chunk_list(cfg["order_in"])):
        if rb is None:
            slot = place // diag
            index = (place % diag) // half
            first = jnp.zeros_like(place)
            second = jnp.zeros_like(place) - 1
            at = 0
            for step in range(1, A):
                for i in range(A - step):
                    first = jnp.where(index == at, i, first)
                    second = jnp.where(index == at, i + step, second)
                    at += 1
            owner = jnp.where(slot == 0, flipped(date, ra), flipped(date, ra + 1))
            want = jnp.where(second >= 0, (owner * A + first) * total + owner * A + second, -2)
        else:
            low, high = pair_order(ra, rb)
            lo_date, hi_date = cfg["place_of"](date, low), cfg["place_of"](date, high)
            first = lo_date * A + place // (A * half)
            second = hi_date * A + (place // half) % A
            want = first * total + second
        hit = jnp.where(code == want, 1.0, 0.0).astype(BF16)
        value = jnp.dot(spread_high, hit, preferred_element_type=F32) + jnp.dot(spread_low, hit, preferred_element_type=F32)
        value = jnp.where(same, value, 0.0)
        columns = slice(n * block, (n + 1) * block)
        k_high[:, columns], k_low[:, columns] = split(value)


def padded(cells, sides, width):
    for axis, dim in sides:
        count = lax.axis_size(axis)
        ends = count - 1
        head = lax.slice_in_dim(cells, 0, width, axis=dim)
        tail = lax.slice_in_dim(cells, cells.shape[dim] - width, cells.shape[dim], axis=dim)
        cells = jnp.concatenate(
            [
                lax.ppermute(tail, axis, [(i, (i + 1) % count) for i in range(ends)]),
                cells,
                lax.ppermute(head, axis, [((i + 1) % count, i) for i in range(ends)]),
            ],
            axis=dim,
        )
    return cells


def look_matrix(padded_width, looks_here):
    column = jnp.arange(padded_width, dtype=jnp.int32)[:, None]
    target = jnp.arange(looks_here, dtype=jnp.int32)[None, :]
    offset = (column - 8 * target).astype(jnp.float32)
    inside = (offset >= 0.0) & (offset < 16.0)
    return jnp.where(inside, (8.0 - jnp.abs(offset - 7.5)) / 64.0, 0.0)


def plain_device(scenes, pair_dates, pair_count, inverse):
    slot_count = pair_dates.shape[0]
    looks_here = scenes.shape[3] // 8
    base = lax.all_to_all(scenes, "date", split_axis=2, concat_axis=0, tiled=True)
    used_dates, used_counts = (
        lax.all_gather(pair_dates, "date", axis=0, tiled=True),
        lax.all_gather(pair_count, "date", axis=0, tiled=True),
    )
    slot_index = jnp.arange(used_dates.shape[0], dtype=jnp.int32)
    living = (slot_index % slot_count < jnp.take(used_counts, slot_index // slot_count)).astype(
        jnp.float32
    )
    primary = jnp.take(base, used_dates[:, 0], axis=0)
    secondary = jnp.take(base, used_dates[:, 1], axis=0)
    p_real = primary[:, 0].astype(jnp.float32)
    p_imag = primary[:, 1].astype(jnp.float32)
    s_real = secondary[:, 0].astype(jnp.float32)
    s_imag = secondary[:, 1].astype(jnp.float32)
    real_part = p_real * s_real + p_imag * s_imag
    imaginary = p_imag * s_real - p_real * s_imag
    products = jnp.stack([real_part, imaginary], axis=1) * living[:, None, None, None]
    products = padded(products, (("col", 3),), 4)
    pair_total = products.shape[0]
    padded_width = products.shape[3]
    half_rows = products.shape[2] // 2
    halved = products.reshape(pair_total, 2, half_rows, 2, padded_width).sum(axis=3) * 0.5
    looked = jnp.dot(
        halved.reshape(-1, padded_width),
        look_matrix(padded_width, looks_here),
        precision=lax.Precision.HIGHEST,
        preferred_element_type=jnp.float32,
    )
    looked = looked.reshape(pair_total, 2, half_rows, looks_here)
    return jnp.einsum("qk,kcrm->qcrm", inverse, looked, precision=lax.Precision.HIGHEST)


def per_device(scenes, pair_dates, pair_count, inverse):
    D, C = lax.axis_size("date"), lax.axis_size("col")
    A, _, rows, X = scenes.shape
    S, NP = pair_dates.shape[0], inverse.shape[0]
    R = rows // D
    half = R // 2
    block = A * A * half
    fits = R % 16 == 0 and X % 128 == 0 and X // 8 <= 64 and D & (D - 1) == 0 and 1 < D and S % 8 == 0 and S <= 128
    fits = fits and block % 128 == 0 and A * (A - 1) // 2 * half <= block // 2 and (block // 2) % 16 == 0 and 8 * 2 * A <= 128
    if not fits or D > 8:
        return plain_device(scenes, pair_dates, pair_count, inverse)
    order_in = list(range(1, D))
    cfg = dict(D=D, C=C, A=A, R=R, X=X, S=S, NP=NP, order_in=order_in, send_order=order_in, place_of=place_of(D))
    total = len(chunk_list(order_in)) * block
    TT = X // 128 + 1
    dma = pltpu.SemaphoreType.DMA
    vmem = pl.BlockSpec(memory_space=pltpu.VMEM)
    return pl.pallas_call(
        functools.partial(stack_kernel, cfg),
        out_shape=pltpu.VMEM((NP, 2, half, X // 8), F32),
        in_specs=[pl.BlockSpec(memory_space=pltpu.HBM)] * 4,
        out_specs=vmem,
        scratch_shapes=[
            pltpu.VMEM(scenes.shape, BF16),
            pltpu.VMEM((D, A, 2, R, X), BF16),
            pltpu.VMEM((D, 2, S), jnp.int32),
            pltpu.VMEM((D, 1, 1), jnp.int32),
            pltpu.VMEM((2, rows, 128), BF16),
            pltpu.VMEM((2, D, R, 128), BF16),
            pltpu.VMEM((2 * TT * A * R, 128), F32),
            pltpu.VMEM((2, 2 * TT, D * A, half, 128), F32),
            pltpu.VMEM((total, 2 * TT * 128), BF16),
            pltpu.VMEM((total, 2 * TT * 128), BF16),
            pltpu.VMEM((2 * TT * 128, 128), BF16),
            pltpu.VMEM((NP * half, total), BF16),
            pltpu.VMEM((NP * half, total), BF16),
            pltpu.VMEM((total, 128), BF16),
            pltpu.VMEM((total, 128), BF16),
            dma, dma((D,)), dma((D,)), dma((D,)), dma((D,)), dma((D,)), dma((D,)), dma((2, D)), dma((2, D)),
            pltpu.VMEM(inverse.shape, F32), dma((3,)),
        ],
        compiler_params=pltpu.CompilerParams(collective_id=0, has_side_effects=True),
    )(scenes, pair_dates.T, pair_count.reshape(1, 1), inverse)


def place_of(D):
    def combine(place, slot):
        out, bit = 0, 1
        while bit < D:
            a, b = (place // bit) % 2, (slot // bit) % 2
            out = out + bit * (a + b - 2 * a * b)
            bit *= 2
        return out
    return combine


def solution(mesh):
    placed = (P("date", None, "groups", "col"), P("date", None), P("date"), P())
    return jax.shard_map(
        per_device,
        mesh=mesh,
        in_specs=placed,
        out_specs=P(None, None, ("groups", "date"), "col"),
        check_vma=False,
    )
```

profile of v0, /device:TPU:0, one launch (start us, length us, event | category | flops | bytes accessed | tf_op | source)
XLA Modules:
  0.0 12.6 jit_solution(11873960463904168398)
XLA Ops:
  0.7 11.3 %shard_map.46 = f32[15,2,8,32]{3,2,1,0:T(8,128)S(1)} custom-call(bf16[4,2,64,256]{3,2,1,0:T(8,128)(2,1)} %scenes.1, s32[2,24]{1,0:T(2,128)} %bitcast.3, s32[1,1]{1,0:T(1,128)} %bitcast.2.count, f32[15,96]{1,0:T(8,128)} %inverse.1), custom_call_target="tpu_custom_call" | custom-call | tf_op jit(solution)/shard_map/pallas_call | solution.py:430
  12.0 0.7 %copy.6 = f32[15,2,8,32]{3,2,1,0:T(8,128)} copy(f32[15,2,8,32]{3,2,1,0:T(8,128)S(1)} %shard_map.46) | data formatting | bytes 61440
where the time goes:
time: 12.8 us; the launch traced here: 12.6 us
  Pallas kernels  11.3 us (88%)
  between operations  0.66 us (5%)
  local copies, waits for them, and re-layouts  0.65 us (5%)
    pallas_call x1, Pallas kernels, per_device(): pl.pallas_call(functools.partial(stack_kernel, cfg), out_shape=pltpu.VMEM...  11.3 us
    unnamed x1, local copies, waits for them, and re-layouts  0.65 us

commit v1 on v0

v1 whole, which is shorter than its diff:
```python
import functools

import jax
import jax.numpy as jnp
from jax import lax
from jax.experimental import pallas as pl
from jax.experimental.pallas import tpu as pltpu
from jax.sharding import PartitionSpec as P

MESH = pl.DeviceIdType.MESH
F32 = jnp.float32
BF16 = jnp.bfloat16
EDGE = 4
LANES = 128
SUBLANES = 8


def flipped(place, slot):
    low, high = place % 2, place // 2
    a, b = slot % 2, slot // 2
    return low + a - 2 * low * a + 2 * (high + b - 2 * high * b)


def split(value):
    high = value.astype(BF16)
    return high, (value - high.astype(F32)).astype(BF16)


def iota(shape, dim):
    return lax.broadcasted_iota(jnp.int32, shape, dim)


def turns(group):
    half = group // 2
    inside = [(g, g, n) for g in range(2) for n in range(1, half + 1)]
    return inside[:half] + [(0, 1, n) for n in range(group)] + inside[half:]


def stack_kernel(
    cfg,
    scenes, dates, count, inverse, out,
    local, near, far, dates_in, counts_in, inverse_in, edge_out, edge_in, turned,
    raw_a, raw_b, raw_e, pairs, pairs_e, weights, coef, along, along_e,
    load_sem, own_sem, far_send, far_recv, near_send, near_recv,
    dates_send, dates_recv, count_send, count_recv, edge_send, edge_recv, met_sem, go_sem,
):
    D, C, A, R, X, S, NP = (cfg[k] for k in ("D", "C", "A", "R", "X", "S", "NP"))
    T = X // LANES
    H = R // SUBLANES
    half = R // 2
    part = SUBLANES // 2
    looks = X // 8
    group = D // 2 * A
    order = turns(group)
    height = len(order) * group
    QP = 2 * SUBLANES
    pitch_a, pitch_b, pitch_r = cfg["pitch_a"], cfg["pitch_b"], cfg["pitch_r"]
    date = lax.axis_index("date")
    col = lax.axis_index("col")
    has_left = col > 0
    has_right = col < C - 1
    leads = date == 0
    sides = has_left.astype(jnp.int32) + has_right.astype(jnp.int32)

    def rows_of(place):
        return pl.ds(pl.multiple_of(place * R, R), R)

    barrier = pltpu.get_barrier_semaphore()
    for r in range(D - 1, 0, -1):
        pl.semaphore_signal(barrier, inc=1, device_id={"date": flipped(date, r)}, device_id_type=MESH)

    load = pltpu.make_async_copy(scenes, local, load_sem)
    load.start()
    own = [
        pltpu.make_async_copy(dates, dates_in.at[date], own_sem.at[0]),
        pltpu.make_async_copy(count, counts_in.at[date], own_sem.at[1]),
        pltpu.make_async_copy(inverse, inverse_in, own_sem.at[2]),
    ]
    for copy in own:
        copy.start()

    @pl.when(leads & has_left)
    def _():
        pl.semaphore_signal(barrier, inc=1, device_id={"col": col - 1}, device_id_type=MESH)

    @pl.when(leads & has_right)
    def _():
        pl.semaphore_signal(barrier, inc=1, device_id={"col": col + 1}, device_id_type=MESH)

    pl.semaphore_wait(barrier, D - 1 + leads.astype(jnp.int32) * sides)

    def remote(src, dst, ssem, rsem, device):
        return pltpu.make_async_remote_copy(src_ref=src, dst_ref=dst, send_sem=ssem, recv_sem=rsem, device_id=device, device_id_type=MESH)

    def chunk(n):
        return n // H, n % H

    def send_far(n):
        t, h = chunk(n)
        for r in (2, 3):
            there = flipped(date, r)
            rows = pl.ds(pl.multiple_of(there * R + h * SUBLANES, SUBLANES), SUBLANES)
            remote(scenes.at[:, :, rows, t * LANES:(t + 1) * LANES], far.at[n, r - 2], far_send, far_recv.at[n], {"date": there}).start()

    send_far(0)
    partner = flipped(date, 1)
    to_near = remote(scenes.at[:, :, rows_of(partner), :], near, near_send, near_recv, {"date": partner})
    to_near.start()
    for r in range(D - 1, 0, -1):
        remote(dates, dates_in.at[date], dates_send, dates_recv, {"date": flipped(date, r)}).start()
        remote(count, counts_in.at[date], count_send, count_recv, {"date": flipped(date, r)}).start()
    for n in range(1, T * H):
        send_far(n)

    @pl.when(leads & has_left)
    def _():
        pl.semaphore_signal(met_sem, inc=1, device_id={"col": col - 1}, device_id_type=MESH)

    @pl.when(leads & has_right)
    def _():
        pl.semaphore_signal(met_sem, inc=1, device_id={"col": col + 1}, device_id_type=MESH)

    @pl.when(jnp.logical_not(has_left))
    def _():
        edge_in[0] = jnp.zeros(edge_in.shape[1:], BF16)

    @pl.when(jnp.logical_not(has_right))
    def _():
        edge_in[1] = jnp.zeros(edge_in.shape[1:], BF16)

    load.wait()
    lane = iota((D * R, LANES), 1)
    packed = jnp.zeros((D * R, LANES), F32)
    for i in range(2 * A):
        first = local[i // 2, i % 2, :, 0:LANES].astype(F32)
        last = local[i // 2, i % 2, :, X - LANES:X].astype(F32)
        shift = 2 * EDGE * i + EDGE
        packed = jnp.where(lane // EDGE == 2 * i, pltpu.roll(last, shift, 1), packed)
        packed = jnp.where(lane // EDGE == 2 * i + 1, pltpu.roll(first, shift, 1), packed)
    packed = jnp.concatenate([packed, jnp.zeros((LANES - D * R, LANES), F32)], axis=0)
    turned[...] = jnp.transpose(packed)
    spot = iota((2 * A, LANES), 1) // R
    columns = [turned[pl.ds(n, 2 * A, stride=2 * EDGE), :] for n in range(2 * EDGE)]
    for side in range(2):
        for d in range(D):
            total = jnp.zeros((2 * A, LANES), F32)
            for n in range(side * EDGE, (side + 1) * EDGE):
                shift = (n * R - d * R) % LANES
                total = jnp.where(spot == n, pltpu.roll(columns[n], shift, 1) if shift else columns[n], total)
            edge_out[side, d] = total.astype(BF16)

    @pl.when(leads)
    def _():
        pl.semaphore_wait(met_sem, sides)
        for r in range(1, D):
            pl.semaphore_signal(go_sem, inc=1, device_id={"date": flipped(date, r)}, device_id_type=MESH)

    @pl.when(jnp.logical_not(leads))
    def _():
        pl.semaphore_wait(go_sem, 1)

    def to_side(side, r):
        there = flipped(date, r)
        return remote(edge_out.at[side, there], edge_in.at[side, r], edge_send.at[side], edge_recv.at[side], {"date": there, "col": col + 1 - 2 * side})

    @pl.when(has_right)
    def _():
        for r in range(D - 1, -1, -1):
            to_side(0, r).start()

    @pl.when(has_left)
    def _():
        for r in range(D - 1, -1, -1):
            to_side(1, r).start()

    row = iota(((T + 1) * LANES, LANES), 0)
    at = row - T * LANES
    place = at // R
    column = jnp.where(at < 0, row, jnp.where(place < EDGE, place - EDGE, place - EDGE + X))
    target = iota(((T + 1) * LANES, LANES), 1)
    offset = column - 8 * target + 4
    inside = (target < looks) & (offset >= 0) & (offset < 16)
    weights[...] = jnp.where(inside, (8.0 - jnp.abs(offset.astype(F32) - 7.5)) / 128.0, 0.0).astype(BF16)

    def unpack(raw, pitch, again, c, t, h, index, block):
        start = ((c * T + t) * R + h * SUBLANES) * pitch + index
        raw[pl.ds(start, SUBLANES, stride=pitch), :] = block
        if index < again:
            raw[pl.ds(start + group, SUBLANES, stride=pitch), :] = block

    def unpack_near(of, slot):
        for c in range(2):
            for t in range(T):
                for i in range(A):
                    both = of(i, c, t).astype(F32)
                    for h in range(H):
                        unpack(raw_a, pitch_a, group // 2, c, t, h, slot * A + i, both[h * SUBLANES:(h + 1) * SUBLANES])

    def got(raw, pitch, c, t, r, parity, turn):
        start = ((c * T + t) * R + 2 * r + parity) * pitch + turn
        return raw[pl.ds(start, group), :]

    def four(raw, pitch, t, r, turn):
        return [got(raw, pitch, c, t, r, parity, turn) for parity in range(2) for c in range(2)]

    def product(p, s):
        real = imaginary = None
        for n in range(0, len(p), 2):
            one = p[n] * s[n] + p[n + 1] * s[n + 1]
            two = p[n + 1] * s[n] - p[n] * s[n + 1]
            real = one if real is None else real + one
            imaginary = two if imaginary is None else imaginary + two
        return real, imaginary

    def emit(into, c, at, lanes, values):
        high, low = split(jnp.concatenate(values, axis=0))
        into[c, at:at + 2 * group, lanes] = high
        into[c, height + at:height + at + 2 * group, lanes] = low

    def run(into, lanes, load_of, steps):
        firsts = {}
        for n in steps:
            both = []
            for g, k, turn in order[2 * n:2 * n + 2]:
                if g not in firsts:
                    firsts[g] = load_of(g, 0)
                both.append(product(firsts[g], load_of(k, turn)))
            for c in range(2):
                emit(into, c, 2 * n * group, lanes, [v[c] for v in both])

    def part_of(n, steps):
        t, h = chunk(n)
        for i in range(part):
            r = h * part + i

            def load_of(g, turn):
                return four(raw_b, pitch_b, t, r, turn) if g else four(raw_a, pitch_a, t, r, turn)

            run(pairs.at[n], slice(i * LANES, (i + 1) * LANES), load_of, steps)

    def contract(c, rhs):
        value = jnp.dot(coef[c], rhs, preferred_element_type=F32)
        return value[0:QP] + value[QP:2 * QP]

    early = group // 4
    steps = len(order) // 2

    unpack_near(lambda i, c, t: local[i, c, rows_of(date), t * LANES:(t + 1) * LANES], 0)
    to_near.wait_recv()
    unpack_near(lambda i, c, t: near[i, c, :, t * LANES:(t + 1) * LANES], 1)
    for n in range(T * H):
        part_of(n, range(early))

    for copy in own:
        copy.wait()
    others = pl.ds(0, D - 1)
    pltpu.make_async_copy(dates_in.at[others], dates_in.at[others], dates_recv).wait()
    pltpu.make_async_copy(counts_in.at[others], counts_in.at[others], count_recv).wait()
    coefficients(cfg, date, order, dates_in, counts_in, inverse_in, coef)

    for n in range(T * H):
        t, h = chunk(n)
        pltpu.make_async_copy(far.at[n], far.at[n], far_recv.at[n]).wait()
        for slot in range(2):
            for i in range(A):
                for c in range(2):
                    unpack(raw_b, pitch_b, group - 1, c, t, h, slot * A + i, far[n, slot, i, c].astype(F32))
        part_of(n, range(early, steps))
        for c in range(2):
            value = contract(c, pairs[n, c])
            for i in range(part):
                start = (h * part + i) * pitch_r + c * QP
                along[t, start:start + QP] = value[:, i * LANES:(i + 1) * LANES]

    @pl.when(has_left)
    def _():
        pltpu.make_async_copy(edge_in.at[0], edge_in.at[0], edge_recv.at[0]).wait()

    @pl.when(has_right)
    def _():
        pltpu.make_async_copy(edge_in.at[1], edge_in.at[1], edge_recv.at[1]).wait()

    for slot in range(D):
        value = edge_in[0, slot].astype(F32) + edge_in[1, slot].astype(F32)
        start = slot // 2 * 4 * group + slot % 2 * 2 * A
        raw_e[start:start + 2 * A] = value
        raw_e[start + 2 * group:start + 2 * group + 2 * A] = value

    def edges_of(g, turn):
        return [raw_e[pl.ds(g * 4 * group + c + 2 * turn, group, stride=2), :] for c in range(2)]

    run(pairs_e, slice(0, LANES), edges_of, range(steps))
    for c in range(2):
        along_e[c * QP:(c + 1) * QP] = contract(c, pairs_e[c])

    mine = (iota((half, LANES), 1) % R) // 2 == iota((half, LANES), 0)
    blocks = []
    for q in range(NP):
        for c in range(2):
            main = [along[t, pl.ds(c * QP + q, half, stride=pitch_r), :] for t in range(T)]
            edge = jnp.where(mine, along_e[pl.ds(c * QP + q, half, stride=0), :], 0.0)
            blocks.append(jnp.concatenate(main + [edge], axis=1))
    high, low = split(jnp.concatenate(blocks, axis=0))
    series = jnp.dot(high, weights[...], preferred_element_type=F32)
    series = series + jnp.dot(low, weights[...], preferred_element_type=F32)
    out[...] = series[:, 0:looks].reshape(NP, 2, half, looks)

    pltpu.make_async_copy(far, far, far_send).wait()
    to_near.wait_send()
    pltpu.make_async_copy(dates_in.at[others], dates_in.at[others], dates_send).wait()
    pltpu.make_async_copy(counts_in.at[others], counts_in.at[others], count_send).wait()

    @pl.when(has_right)
    def _():
        pltpu.make_async_copy(edge_out.at[0], edge_out.at[0], edge_send.at[0]).wait()

    @pl.when(has_left)
    def _():
        pltpu.make_async_copy(edge_out.at[1], edge_out.at[1], edge_send.at[1]).wait()


def coefficients(cfg, date, order, dates_in, counts_in, inverse, coef):
    D, A, S, NP = (cfg[k] for k in ("D", "A", "S", "NP"))
    total = D * A
    group = D // 2 * A
    height = len(order) * group
    codes = []
    for d in range(D):
        row = dates_in[d, 0:1, :] * total + dates_in[d, 1:2, :]
        live = iota((1, S), 1) < counts_in[d]
        codes.append(jnp.where(live, row, -1).astype(F32))
    codes.append(jnp.full((SUBLANES - D, S), -1.0, F32))
    table = jnp.concatenate(codes, axis=0)
    table = jnp.concatenate([table, jnp.full((SUBLANES, LANES - S), -1.0, F32)], axis=1)
    spun = jnp.transpose(table)
    code = jnp.concatenate([spun[0:S, d:d + 1] for d in range(D)], axis=0).astype(jnp.int32)

    place = iota((1, height), 1)
    index = place % group
    first, second, valid = index, index, index >= 0
    for n, (g, k, turn) in enumerate(order):
        here = place // group == n
        first = jnp.where(here, g * group + index, first)
        second = jnp.where(here, k * group + (index + turn) % group, second)
        if g == k and 2 * turn == group:
            valid = valid & jnp.logical_not(here & (index >= turn))
    first = flipped(date, first // A) * A + first % A
    second = flipped(date, second // A) * A + second % A
    ahead = first < second
    want = jnp.where(ahead, first * total + second, second * total + first)
    want = jnp.where(valid, want, -2)
    hit = jnp.where(code == want, 1.0, 0.0).astype(BF16)
    high, low = split(jnp.concatenate([inverse[...], jnp.zeros((2 * SUBLANES - NP, D * S), F32)], axis=0))
    value = jnp.dot(high, hit, preferred_element_type=F32) + jnp.dot(low, hit, preferred_element_type=F32)
    for c in range(2):
        high, low = split(value if c == 0 else jnp.where(ahead, value, -value))
        top = jnp.concatenate([high, high], axis=1)
        bottom = jnp.concatenate([low, jnp.zeros_like(low)], axis=1)
        coef[c] = jnp.concatenate([top, bottom], axis=0)


def padded(cells, sides, width):
    for axis, dim in sides:
        count = lax.axis_size(axis)
        ends = count - 1
        head = lax.slice_in_dim(cells, 0, width, axis=dim)
        tail = lax.slice_in_dim(cells, cells.shape[dim] - width, cells.shape[dim], axis=dim)
        cells = jnp.concatenate(
            [
                lax.ppermute(tail, axis, [(i, (i + 1) % count) for i in range(ends)]),
                cells,
                lax.ppermute(head, axis, [((i + 1) % count, i) for i in range(ends)]),
            ],
            axis=dim,
        )
    return cells


def look_matrix(padded_width, looks_here):
    column = jnp.arange(padded_width, dtype=jnp.int32)[:, None]
    target = jnp.arange(looks_here, dtype=jnp.int32)[None, :]
    offset = (column - 8 * target).astype(jnp.float32)
    inside = (offset >= 0.0) & (offset < 16.0)
    return jnp.where(inside, (8.0 - jnp.abs(offset - 7.5)) / 64.0, 0.0)


def plain_device(scenes, pair_dates, pair_count, inverse):
    slot_count = pair_dates.shape[0]
    looks_here = scenes.shape[3] // 8
    base = lax.all_to_all(scenes, "date", split_axis=2, concat_axis=0, tiled=True)
    used_dates, used_counts = (
        lax.all_gather(pair_dates, "date", axis=0, tiled=True),
        lax.all_gather(pair_count, "date", axis=0, tiled=True),
    )
    slot_index = jnp.arange(used_dates.shape[0], dtype=jnp.int32)
    living = (slot_index % slot_count < jnp.take(used_counts, slot_index // slot_count)).astype(
        jnp.float32
    )
    primary = jnp.take(base, used_dates[:, 0], axis=0)
    secondary = jnp.take(base, used_dates[:, 1], axis=0)
    p_real = primary[:, 0].astype(jnp.float32)
    p_imag = primary[:, 1].astype(jnp.float32)
    s_real = secondary[:, 0].astype(jnp.float32)
    s_imag = secondary[:, 1].astype(jnp.float32)
    real_part = p_real * s_real + p_imag * s_imag
    imaginary = p_imag * s_real - p_real * s_imag
    products = jnp.stack([real_part, imaginary], axis=1) * living[:, None, None, None]
    products = padded(products, (("col", 3),), 4)
    pair_total = products.shape[0]
    padded_width = products.shape[3]
    half_rows = products.shape[2] // 2
    halved = products.reshape(pair_total, 2, half_rows, 2, padded_width).sum(axis=3) * 0.5
    looked = jnp.dot(
        halved.reshape(-1, padded_width),
        look_matrix(padded_width, looks_here),
        precision=lax.Precision.HIGHEST,
        preferred_element_type=jnp.float32,
    )
    looked = looked.reshape(pair_total, 2, half_rows, looks_here)
    return jnp.einsum("qk,kcrm->qcrm", inverse, looked, precision=lax.Precision.HIGHEST)


def per_device(scenes, pair_dates, pair_count, inverse):
    D, C = lax.axis_size("date"), lax.axis_size("col")
    A, _, rows, X = scenes.shape
    S, NP = pair_dates.shape[0], inverse.shape[0]
    R = rows // D
    half = R // 2
    fits = D == 4 and 2 * A == SUBLANES and R == 2 * SUBLANES and X % LANES == 0 and X // 8 <= LANES and X <= 4 * LANES
    fits = fits and S % 8 == 0 and S <= LANES and NP <= 2 * SUBLANES and rows <= LANES
    if not fits:
        return plain_device(scenes, pair_dates, pair_count, inverse)
    T, H = X // LANES, R // SUBLANES
    group = D // 2 * A
    height = len(turns(group)) * group
    cfg = dict(D=D, C=C, A=A, R=R, X=X, S=S, NP=NP, pitch_a=group + group // 2 + 1, pitch_b=2 * group - 1, pitch_r=4 * SUBLANES + 1)
    dma, regular = pltpu.SemaphoreType.DMA, pltpu.SemaphoreType.REGULAR
    return pl.pallas_call(
        functools.partial(stack_kernel, cfg),
        out_shape=pltpu.VMEM((NP, 2, half, X // 8), F32),
        in_specs=[pl.BlockSpec(memory_space=pltpu.HBM)] * 4,
        out_specs=pl.BlockSpec(memory_space=pltpu.VMEM),
        scratch_shapes=[
            pltpu.VMEM(scenes.shape, BF16),
            pltpu.VMEM((A, 2, R, X), BF16),
            pltpu.VMEM((T * H, 2, A, 2, SUBLANES, LANES), BF16),
            pltpu.VMEM((D, 2, S), jnp.int32),
            pltpu.VMEM((D, 1, 1), jnp.int32),
            pltpu.VMEM(inverse.shape, F32),
            pltpu.VMEM((2, D, 2 * A, LANES), BF16),
            pltpu.VMEM((2, D, 2 * A, LANES), BF16),
            pltpu.VMEM((LANES, LANES), F32),
            pltpu.VMEM((2 * T * R * cfg["pitch_a"], LANES), F32),
            pltpu.VMEM((2 * T * R * cfg["pitch_b"], LANES), F32),
            pltpu.VMEM((8 * group, LANES), F32),
            pltpu.VMEM((T * H, 2, 2 * height, SUBLANES // 2 * LANES), BF16),
            pltpu.VMEM((2, 2 * height, LANES), BF16),
            pltpu.VMEM(((T + 1) * LANES, LANES), BF16),
            pltpu.VMEM((2, 4 * SUBLANES, 2 * height), BF16),
            pltpu.VMEM((T, half * cfg["pitch_r"], LANES), F32),
            pltpu.VMEM((4 * SUBLANES, LANES), F32),
            dma, dma((3,)), dma, dma((T * H,)), dma, dma,
            dma, dma, dma, dma, dma((2,)), dma((2,)), regular, regular,
        ],
        compiler_params=pltpu.CompilerParams(collective_id=0, has_side_effects=True),
    )(scenes, pair_dates.T, pair_count.reshape(1, 1), inverse)


def solution(mesh):
    placed = (P("date", None, "groups", "col"), P("date", None), P("date"), P())
    return jax.shard_map(
        per_device,
        mesh=mesh,
        in_specs=placed,
        out_specs=P(None, None, ("groups", "date"), "col"),
        check_vma=False,
    )
```

time: 12.8 us -> 11.5 us (0.90)
  Pallas kernels: 11.3 us -> 10 us
    pallas_call x1, Pallas kernels: 11.3 us -> 10 us  [per_device(): pl.pallas_call(functools.partial(stack_kernel, cfg), out_shape=pltpu.VMEM...]
where the time goes in v1:
time: 11.5 us; the launch traced here: 11.3 us
  Pallas kernels  10 us (87%)
  between operations  0.66 us (6%)
  local copies, waits for them, and re-layouts  0.65 us (6%)
    pallas_call x1, Pallas kernels, per_device(): pl.pallas_call(functools.partial(stack_kernel, cfg), out_shape=pltpu.VMEM...  10 us
    unnamed x1, local copies, waits for them, and re-layouts  0.65 us

profile of v1, /device:TPU:0, one launch (start us, length us, event | category | flops | bytes accessed | tf_op | source)
XLA Modules:
  0.0 11.3 jit_solution(11048790046947245436)
XLA Ops:
  0.7 10.0 %shard_map.46 = f32[15,2,8,32]{3,2,1,0:T(8,128)S(1)} custom-call(bf16[4,2,64,256]{3,2,1,0:T(8,128)(2,1)} %scenes.1, s32[2,24]{1,0:T(2,128)} %bitcast.3, s32[1,1]{1,0:T(1,128)} %bitcast.2.count, f32[15,96]{1,0:T(8,128)} %inverse.1), custom_call_target="tpu_custom_call" | custom-call | tf_op jit(solution)/shard_map/pallas_call | solution.py:438
  10.7 0.7 %copy.6 = f32[15,2,8,32]{3,2,1,0:T(8,128)} copy(f32[15,2,8,32]{3,2,1,0:T(8,128)S(1)} %shard_map.46) | data formatting | bytes 61440

commit v2 on v1

--- a/solution.py
+++ b/solution.py
@@ -42,13 +42,15 @@
     local, near, far, dates_in, counts_in, inverse_in, edge_out, edge_in, turned,
     raw_a, raw_b, raw_e, pairs, pairs_e, weights, coef, along, along_e,
     load_sem, own_sem, far_send, far_recv, near_send, near_recv,
-    dates_send, dates_recv, count_send, count_recv, edge_send, edge_recv, met_sem, go_sem,
+    dates_send, dates_recv, count_send, count_recv, edge_send, edge_recv, met_sem,
 ):
     D, C, A, R, X, S, NP = (cfg[k] for k in ("D", "C", "A", "R", "X", "S", "NP"))
     T = X // LANES
     H = R // SUBLANES
     half = R // 2
     part = SUBLANES // 2
+    W = cfg["W"]
+    K = T // W * H
     looks = X // 8
     group = D // 2 * A
     order = turns(group)
@@ -59,7 +61,7 @@
     col = lax.axis_index("col")
     has_left = col > 0
     has_right = col < C - 1
-    leads = date == 0
+    odd = col % 2 == 1
     sides = has_left.astype(jnp.int32) + has_right.astype(jnp.int32)
 
     def rows_of(place):
@@ -68,6 +70,16 @@
     barrier = pltpu.get_barrier_semaphore()
     for r in range(D - 1, 0, -1):
         pl.semaphore_signal(barrier, inc=1, device_id={"date": flipped(date, r)}, device_id_type=MESH)
+
+    @pl.when(jnp.logical_not(odd) & has_right)
+    def _():
+        for r in range(D - 1, -1, -1):
+            pl.semaphore_signal(barrier, inc=1, device_id={"date": flipped(date, r), "col": col + 1}, device_id_type=MESH)
+
+    @pl.when(jnp.logical_not(odd) & has_left)
+    def _():
+        for r in range(D - 1, -1, -1):
+            pl.semaphore_signal(barrier, inc=1, device_id={"date": flipped(date, r), "col": col - 1}, device_id_type=MESH)
 
     load = pltpu.make_async_copy(scenes, local, load_sem)
     load.start()
@@ -79,46 +91,35 @@
     for copy in own:
         copy.start()
 
-    @pl.when(leads & has_left)
-    def _():
-        pl.semaphore_signal(barrier, inc=1, device_id={"col": col - 1}, device_id_type=MESH)
-
-    @pl.when(leads & has_right)
-    def _():
-        pl.semaphore_signal(barrier, inc=1, device_id={"col": col + 1}, device_id_type=MESH)
-
-    pl.semaphore_wait(barrier, D - 1 + leads.astype(jnp.int32) * sides)
-
     def remote(src, dst, ssem, rsem, device):
         return pltpu.make_async_remote_copy(src_ref=src, dst_ref=dst, send_sem=ssem, recv_sem=rsem, device_id=device, device_id_type=MESH)
 
     def chunk(n):
-        return n // H, n % H
+        return n // H * W, n % H
 
     def send_far(n):
         t, h = chunk(n)
         for r in (2, 3):
             there = flipped(date, r)
             rows = pl.ds(pl.multiple_of(there * R + h * SUBLANES, SUBLANES), SUBLANES)
-            remote(scenes.at[:, :, rows, t * LANES:(t + 1) * LANES], far.at[n, r - 2], far_send, far_recv.at[n], {"date": there}).start()
-
-    send_far(0)
+            remote(scenes.at[:, :, rows, t * LANES:(t + W) * LANES], far.at[n, r - 2], far_send, far_recv.at[n], {"date": there}).start()
+
     partner = flipped(date, 1)
     to_near = remote(scenes.at[:, :, rows_of(partner), :], near, near_send, near_recv, {"date": partner})
-    to_near.start()
-    for r in range(D - 1, 0, -1):
-        remote(dates, dates_in.at[date], dates_send, dates_recv, {"date": flipped(date, r)}).start()
-        remote(count, counts_in.at[date], count_send, count_recv, {"date": flipped(date, r)}).start()
-    for n in range(1, T * H):
-        send_far(n)
-
-    @pl.when(leads & has_left)
-    def _():
-        pl.semaphore_signal(met_sem, inc=1, device_id={"col": col - 1}, device_id_type=MESH)
-
-    @pl.when(leads & has_right)
-    def _():
-        pl.semaphore_signal(met_sem, inc=1, device_id={"col": col + 1}, device_id_type=MESH)
+
+    def send_scenes():
+        send_far(0)
+        to_near.start()
+        for r in range(D - 1, 0, -1):
+            remote(dates, dates_in.at[date], dates_send, dates_recv, {"date": flipped(date, r)}).start()
+            remote(count, counts_in.at[date], count_send, count_recv, {"date": flipped(date, r)}).start()
+        for n in range(1, K):
+            send_far(n)
+
+    @pl.when(jnp.logical_not(odd))
+    def _():
+        pl.semaphore_wait(barrier, D - 1)
+        send_scenes()
 
     @pl.when(jnp.logical_not(has_left))
     def _():
@@ -149,29 +150,38 @@
                 total = jnp.where(spot == n, pltpu.roll(columns[n], shift, 1) if shift else columns[n], total)
             edge_out[side, d] = total.astype(BF16)
 
-    @pl.when(leads)
-    def _():
-        pl.semaphore_wait(met_sem, sides)
-        for r in range(1, D):
-            pl.semaphore_signal(go_sem, inc=1, device_id={"date": flipped(date, r)}, device_id_type=MESH)
-
-    @pl.when(jnp.logical_not(leads))
-    def _():
-        pl.semaphore_wait(go_sem, 1)
-
     def to_side(side, r):
         there = flipped(date, r)
         return remote(edge_out.at[side, there], edge_in.at[side, r], edge_send.at[side], edge_recv.at[side], {"date": there, "col": col + 1 - 2 * side})
 
-    @pl.when(has_right)
-    def _():
-        for r in range(D - 1, -1, -1):
-            to_side(0, r).start()
-
-    @pl.when(has_left)
-    def _():
-        for r in range(D - 1, -1, -1):
-            to_side(1, r).start()
+    def send_edges(chosen):
+        @pl.when(chosen & has_right)
+        def _():
+            for r in range(D - 1, -1, -1):
+                to_side(0, r).start()
+
+        @pl.when(chosen & has_left)
+        def _():
+            for r in range(D - 1, -1, -1):
+                to_side(1, r).start()
+
+    @pl.when(odd)
+    def _():
+        pl.semaphore_wait(barrier, D - 1 + D * sides)
+
+    @pl.when(odd & has_left)
+    def _():
+        pl.semaphore_signal(met_sem, inc=1, device_id={"col": col - 1}, device_id_type=MESH)
+
+    @pl.when(odd & has_right)
+    def _():
+        pl.semaphore_signal(met_sem, inc=1, device_id={"col": col + 1}, device_id_type=MESH)
+
+    send_edges(odd)
+
+    @pl.when(odd)
+    def _():
+        send_scenes()
 
     row = iota(((T + 1) * LANES, LANES), 0)
     at = row - T * LANES
@@ -230,13 +240,15 @@
 
     def part_of(n, steps):
         t, h = chunk(n)
-        for i in range(part):
-            r = h * part + i
-
-            def load_of(g, turn):
-                return four(raw_b, pitch_b, t, r, turn) if g else four(raw_a, pitch_a, t, r, turn)
-
-            run(pairs.at[n], slice(i * LANES, (i + 1) * LANES), load_of, steps)
+        for u in range(W):
+            for i in range(part):
+                r = h * part + i
+
+                def load_of(g, turn):
+                    return four(raw_b, pitch_b, t + u, r, turn) if g else four(raw_a, pitch_a, t + u, r, turn)
+
+                at = (u * part + i) * LANES
+                run(pairs.at[n], slice(at, at + LANES), load_of, steps)
 
     def contract(c, rhs):
         value = jnp.dot(coef[c], rhs, preferred_element_type=F32)
@@ -246,9 +258,15 @@
     steps = len(order) // 2
 
     unpack_near(lambda i, c, t: local[i, c, rows_of(date), t * LANES:(t + 1) * LANES], 0)
+    @pl.when(jnp.logical_not(odd))
+    def _():
+        pl.semaphore_wait(met_sem, sides)
+
+    send_edges(jnp.logical_not(odd))
+
     to_near.wait_recv()
     unpack_near(lambda i, c, t: near[i, c, :, t * LANES:(t + 1) * LANES], 1)
-    for n in range(T * H):
+    for n in range(K):
         part_of(n, range(early))
 
     for copy in own:
@@ -258,19 +276,23 @@
     pltpu.make_async_copy(counts_in.at[others], counts_in.at[others], count_recv).wait()
     coefficients(cfg, date, order, dates_in, counts_in, inverse_in, coef)
 
-    for n in range(T * H):
+    for n in range(K):
         t, h = chunk(n)
         pltpu.make_async_copy(far.at[n], far.at[n], far_recv.at[n]).wait()
         for slot in range(2):
             for i in range(A):
                 for c in range(2):
-                    unpack(raw_b, pitch_b, group - 1, c, t, h, slot * A + i, far[n, slot, i, c].astype(F32))
+                    for u in range(W):
+                        block = far[n, slot, i, c, :, u * LANES:(u + 1) * LANES].astype(F32)
+                        unpack(raw_b, pitch_b, group - 1, c, t + u, h, slot * A + i, block)
         part_of(n, range(early, steps))
         for c in range(2):
             value = contract(c, pairs[n, c])
-            for i in range(part):
-                start = (h * part + i) * pitch_r + c * QP
-                along[t, start:start + QP] = value[:, i * LANES:(i + 1) * LANES]
+            for u in range(W):
+                for i in range(part):
+                    start = (h * part + i) * pitch_r + c * QP
+                    at = (u * part + i) * LANES
+                    along[t + u, start:start + QP] = value[:, at:at + LANES]
 
     @pl.when(has_left)
     def _():
@@ -431,9 +453,11 @@
     if not fits:
         return plain_device(scenes, pair_dates, pair_count, inverse)
     T, H = X // LANES, R // SUBLANES
+    W = 1
+    K = T // W * H
     group = D // 2 * A
     height = len(turns(group)) * group
-    cfg = dict(D=D, C=C, A=A, R=R, X=X, S=S, NP=NP, pitch_a=group + group // 2 + 1, pitch_b=2 * group - 1, pitch_r=4 * SUBLANES + 1)
+    cfg = dict(D=D, C=C, A=A, R=R, X=X, S=S, NP=NP, pitch_a=group + group // 2 + 1, pitch_b=2 * group - 1, pitch_r=4 * SUBLANES + 1, W=W)
     dma, regular = pltpu.SemaphoreType.DMA, pltpu.SemaphoreType.REGULAR
     return pl.pallas_call(
         functools.partial(stack_kernel, cfg),
@@ -443,7 +467,7 @@
         scratch_shapes=[
             pltpu.VMEM(scenes.shape, BF16),
             pltpu.VMEM((A, 2, R, X), BF16),
-            pltpu.VMEM((T * H, 2, A, 2, SUBLANES, LANES), BF16),
+            pltpu.VMEM((K, 2, A, 2, SUBLANES, W * LANES), BF16),
             pltpu.VMEM((D, 2, S), jnp.int32),
             pltpu.VMEM((D, 1, 1), jnp.int32),
             pltpu.VMEM(inverse.shape, F32),
@@ -453,14 +477,14 @@
             pltpu.VMEM((2 * T * R * cfg["pitch_a"], LANES), F32),
             pltpu.VMEM((2 * T * R * cfg["pitch_b"], LANES), F32),
             pltpu.VMEM((8 * group, LANES), F32),
-            pltpu.VMEM((T * H, 2, 2 * height, SUBLANES // 2 * LANES), BF16),
+            pltpu.VMEM((K, 2, 2 * height, SUBLANES // 2 * W * LANES), BF16),
             pltpu.VMEM((2, 2 * height, LANES), BF16),
             pltpu.VMEM(((T + 1) * LANES, LANES), BF16),
             pltpu.VMEM((2, 4 * SUBLANES, 2 * height), BF16),
             pltpu.VMEM((T, half * cfg["pitch_r"], LANES), F32),
             pltpu.VMEM((4 * SUBLANES, LANES), F32),
-            dma, dma((3,)), dma, dma((T * H,)), dma, dma,
-            dma, dma, dma, dma, dma((2,)), dma((2,)), regular, regular,
+            dma, dma((3,)), dma, dma((K,)), dma, dma,
+            dma, dma, dma, dma, dma((2,)), dma((2,)), regular,
         ],
         compiler_params=pltpu.CompilerParams(collective_id=0, has_side_effects=True),
     )(scenes, pair_dates.T, pair_count.reshape(1, 1), inverse)

time: 11.5 us -> 10.1 us (0.88)
  the two profiles are of different devices: /device:TPU:0 before, /device:TPU:9 now
where the time goes in v2:
time: 10.1 us; the launch traced here: 9.98 us
  Pallas kernels  8.67 us (86%)
  between operations  0.66 us (7%)
  local copies, waits for them, and re-layouts  0.65 us (6%)
    pallas_call x1, Pallas kernels, per_device(): pl.pallas_call(functools.partial(stack_kernel, cfg), out_shape=pltpu.VMEM...  8.67 us
    unnamed x1, local copies, waits for them, and re-layouts  0.65 us

profile of v2, /device:TPU:9, one launch (start us, length us, event | category | flops | bytes accessed | tf_op | source)
XLA Modules:
  0.0 10.0 jit_solution(12701919243049869900)
XLA Ops:
  0.7 8.7 %shard_map.46 = f32[15,2,8,32]{3,2,1,0:T(8,128)S(1)} custom-call(bf16[4,2,64,256]{3,2,1,0:T(8,128)(2,1)} %scenes.1, s32[2,24]{1,0:T(2,128)} %bitcast.3, s32[1,1]{1,0:T(1,128)} %bitcast.2.count, f32[15,96]{1,0:T(8,128)} %inverse.1), custom_call_target="tpu_custom_call" | custom-call | tf_op jit(solution)/shard_map/pallas_call | solution.py:462
  9.3 0.7 %copy.6 = f32[15,2,8,32]{3,2,1,0:T(8,128)} copy(f32[15,2,8,32]{3,2,1,0:T(8,128)S(1)} %shard_map.46) | data formatting | bytes 61440

commit v3 on v2

--- a/solution.py
+++ b/solution.py
@@ -102,7 +102,9 @@
         for r in (2, 3):
             there = flipped(date, r)
             rows = pl.ds(pl.multiple_of(there * R + h * SUBLANES, SUBLANES), SUBLANES)
-            remote(scenes.at[:, :, rows, t * LANES:(t + W) * LANES], far.at[n, r - 2], far_send, far_recv.at[n], {"date": there}).start()
+            for i in range(A):
+                some = slice(i, i + 1)
+                remote(scenes.at[some, :, rows, t * LANES:(t + W) * LANES], far.at[n, r - 2, some], far_send, far_recv.at[n], {"date": there}).start()
 
     partner = flipped(date, 1)
     to_near = remote(scenes.at[:, :, rows_of(partner), :], near, near_send, near_recv, {"date": partner})
@@ -323,8 +325,8 @@
             edge = jnp.where(mine, along_e[pl.ds(c * QP + q, half, stride=0), :], 0.0)
             blocks.append(jnp.concatenate(main + [edge], axis=1))
     high, low = split(jnp.concatenate(blocks, axis=0))
-    series = jnp.dot(high, weights[...], preferred_element_type=F32)
-    series = series + jnp.dot(low, weights[...], preferred_element_type=F32)
+    both = jnp.dot(jnp.concatenate([high, low], axis=0), weights[...], preferred_element_type=F32)
+    series = both[0:2 * NP * half] + both[2 * NP * half:]
     out[...] = series[:, 0:looks].reshape(NP, 2, half, looks)
 
     pltpu.make_async_copy(far, far, far_send).wait()

time: 10.1 us -> 10.1 us (level)
  the two profiles are of different devices: /device:TPU:9 before, /device:TPU:13 now
where the time goes in v3:
time: 10.1 us; the launch traced here: 9.91 us
  Pallas kernels  8.6 us (85%)
  between operations  0.66 us (7%)
  local copies, waits for them, and re-layouts  0.65 us (6%)
    pallas_call x1, Pallas kernels, per_device(): pl.pallas_call(functools.partial(stack_kernel, cfg), out_shape=pltpu.VMEM...  8.6 us
    unnamed x1, local copies, waits for them, and re-layouts  0.65 us

profile of v3, /device:TPU:13, one launch (start us, length us, event | category | flops | bytes accessed | tf_op | source)
XLA Modules:
  0.0 9.9 jit_solution(6593795998708130652)
XLA Ops:
  0.7 8.6 %shard_map.46 = f32[15,2,8,32]{3,2,1,0:T(8,128)S(1)} custom-call(bf16[4,2,64,256]{3,2,1,0:T(8,128)(2,1)} %scenes.1, s32[2,24]{1,0:T(2,128)} %bitcast.3, s32[1,1]{1,0:T(1,128)} %bitcast.2.count, f32[15,96]{1,0:T(8,128)} %inverse.1), custom_call_target="tpu_custom_call" | custom-call | tf_op jit(solution)/shard_map/pallas_call | solution.py:464
  9.3 0.7 %copy.6 = f32[15,2,8,32]{3,2,1,0:T(8,128)} copy(f32[15,2,8,32]{3,2,1,0:T(8,128)S(1)} %shard_map.46) | data formatting | bytes 61440
